TPU v7x, 128 devices: a whole 4x4x4 slice. The times are simulated.
128 devices in a mesh: row: 16 (over y, x), col: 8 (over z, core).
Axes of the slice: x: 4, y: 4, z: 4, core: 2. Of those that a mesh axis runs over, the one named last changes fastest.
Arguments:
- orbitals: float32 [32768, 1024], P('row', 'col'), may hold values from -6 to 6
- point_index: int32 [8192], replicated, may hold values from 0 to 32767, as said below
- coulomb: float32 [8192, 8192], P('row', 'col'), may hold values from -0.001953125 to 0.001953125
- fitting: float32 [32768, 8192], P('row', 'col'), may hold values from -0.0625 to 0.0625
Outputs:
- exchange_out: float32 [32768, 1024], P('row', 'col')
Inputs may be any that keep to these rules, and one draw needn't show every extreme that they name: `point_index`: indices are distinct. Grid index g lies in slab g // 2048. Of the 512 consecutive points of each row panel, at most 64 lie in one slab, and in every panel exactly 64 lie in one slab.
All inputs are finite; a program needn't handle non-finite values.
Results may differ from a plain program's by a relative error of at most 0.00012.
Values sent between devices are 32-bit elements; how exact they have to be, the bound alone decides.
No kernel may reach another device: no remote copies, remote signals or barrier semaphores. Data moves between devices by JAX's collectives and lax.ppermute only.
A program may use at most 64 MiB of HBM per device.

v0:
```python
import jax
import jax.numpy as jnp
from jax import lax
from jax.sharding import PartitionSpec as P


def per_device(orbitals, point_index, coulomb, fitting):
    row_count = lax.axis_size("row")
    slab_rows = orbitals.shape[0]
    band_cols = orbitals.shape[1]
    total_points = point_index.shape[0]
    per_panel = total_points // row_count
    slot_count = 2 * per_panel // row_count
    my_row = lax.axis_index("row")
    my_col = lax.axis_index("col")
    owner = point_index // slab_rows
    local_row = point_index - owner * slab_rows
    owner_grid = owner.reshape(row_count, per_panel)
    local_grid = local_row.reshape(row_count, per_panel)
    matches = (owner_grid[:, :, None] == jnp.arange(row_count)[None, None, :]).astype(jnp.int32)
    ranking = jnp.cumsum(matches, axis=1) - 1
    slot_grid = jnp.sum(jnp.where(matches > 0, ranking, 0), axis=2)
    mine = owner_grid == my_row
    chosen = mine[:, :, None] & (slot_grid[:, :, None] == jnp.arange(slot_count)[None, None, :])
    source_row = jnp.sum(jnp.where(chosen, local_grid[:, :, None], 0), axis=1)
    valid = jnp.any(chosen, axis=1)
    outgoing = jnp.where(valid[:, :, None], orbitals[source_row], 0.0)
    received = lax.all_to_all(outgoing, "row", split_axis=0, concat_axis=0, tiled=True)
    flattened = received.reshape(row_count * slot_count, band_cols)
    owner_mine = lax.dynamic_slice_in_dim(owner_grid, my_row, 1, 0)[0]
    slot_mine = lax.dynamic_slice_in_dim(slot_grid, my_row, 1, 0)[0]
    panel_strip = flattened[owner_mine * slot_count + slot_mine]
    panel_full = lax.all_gather(panel_strip, "col", axis=1, tiled=True)
    strip_all = lax.all_gather(panel_strip, "row", axis=0, tiled=True)
    column_full = lax.all_to_all(strip_all, "col", split_axis=0, concat_axis=1, tiled=True)
    pair = jnp.dot(
        panel_full,
        column_full.T,
        precision=lax.Precision.HIGHEST,
        preferred_element_type=jnp.float32,
    )
    partial_value = jnp.dot(
        coulomb * pair,
        column_full,
        precision=lax.Precision.HIGHEST,
        preferred_element_type=jnp.float32,
    )
    summed = lax.psum(partial_value, "col")
    weight_strip = lax.dynamic_slice_in_dim(summed, my_col * band_cols, band_cols, 1)
    weight_all = lax.all_gather(weight_strip, "row", axis=0, tiled=True)
    weight_column = lax.all_to_all(weight_all, "col", split_axis=0, concat_axis=1, tiled=True)
    term = -jnp.dot(
        fitting, weight_column, precision=lax.Precision.HIGHEST, preferred_element_type=jnp.float32
    )
    return lax.psum_scatter(term, "col", scatter_dimension=1, tiled=True)


def solution(mesh):
    in_specs = (P("row", "col"), P(), P("row", "col"), P("row", "col"))
    out_specs = P("row", "col")
    return jax.shard_map(
        per_device, mesh=mesh, in_specs=in_specs, out_specs=out_specs, check_vma=False
    )
```

profile of v0, /device:TPU:1, one launch (start us, length us, event | category | flops | bytes accessed | tf_op | source)
XLA Modules:
  0.0 455.0 jit_solution(17053227646644260959)
XLA Ops:
  6.5 0.0 copy-start
  6.5 0.9 add_select_fusion
  7.4 0.1 fusion.6
  7.5 18.1 %reduce-window.6 = s32[16,16,4,128]{3,1,2,0:T(8,128)S(1)} reduce-window(s32[16,16,4,128]{3,1,2,0:T(8,128)S(1)} %fusion.6, s32[]{:T(128)} %constant.16.clone.1), window={size=1x1x1x128 pad=0_0x0_0x0_0x127_0}, to_apply=%region_0.1 | reduce-window | flops 16646144 | bytes 1048580 | tf_op jit(solution)/shard_map/reduce-window
  25.6 0.2 slice.12
  25.9 0.4 copy.12
  26.3 0.1 fusion.8
  26.5 0.2 fusion.5
  26.7 0.4 fusion.3
  27.1 0.5 select_reduce_fusion
  27.7 0.1 reshape.84
  27.7 0.0 copy-done
  27.7 2.8 gather_fusion
  30.6 1.0 broadcast_select_fusion
  31.6 7.6 %all-to-all-start = ((f32[16,64,128]{2,1,0:T(8,128)}), f32[16,64,128]{2,1,0:T(8,128)S(1)}, u32[]{:S(2)}, u32[]{:S(2)}) async-start(f32[16,64,128]{2,1,0:T(8,128)} %broadcast_select_fusion), calls=%async_computation | async-start | bytes 1048576 | tf_op jit(solution)/shard_map/all_to_all | solution.py:28
  39.1 0.0 all-gather.10.cloned.1.call-start
  39.2 10.3 %all-to-all-done = f32[16,64,128]{2,1,0:T(8,128)S(1)} async-done(((f32[16,64,128]{2,1,0:T(8,128)}), f32[16,64,128]{2,1,0:T(8,128)S(1)}, u32[]{:S(2)}, u32[]{:S(2)}) %all-to-all-start) | async-done | bytes 524320 | tf_op jit(solution)/shard_map/all_to_all | solution.py:28
  49.6 1.6 gather_fusion.1
  51.2 0.0 all-gather.10.cloned.1.call-update
  51.2 0.0 all-gather.8.cloned.1.call-start
  51.3 0.7 all-gather.8.cloned.1.call-update
  52.0 50.4 %all-gather.10.cloned.1.call-done = f32[8192,128]{1,0:T(8,128)} async-done(((f32[512,128]{1,0:T(8,128)}), f32[8192,128]{1,0:T(8,128)}) %all-gather.10.cloned.1.call-update) | async-done | bytes 4194320 | tf_op jit(solution)/shard_map/all_gather | solution.py:34
  102.4 5.4 %copy.15 = f32[8,1024,128]{1,2,0:T(8,128)} copy(f32[8,1024,128]{2,1,0:T(8,128)} %bitcast.44) | data formatting | bytes 8388608 | tf_op jit(solution)/shard_map/all_to_all | solution.py:35
  107.7 5.3 %all-to-all-start.1 = ((f32[8,1024,128]{1,2,0:T(8,128)}), f32[8,1024,128]{1,2,0:T(8,128)}, u32[]{:S(2)}, u32[]{:S(2)}) async-start(f32[8,1024,128]{1,2,0:T(8,128)} %copy.15), calls=%async_computation.1 | async-start | bytes 8388608 | tf_op jit(solution)/shard_map/all_to_all | solution.py:35
  113.0 0.0 all-reduce.2.cloned.1.call-start
  113.0 31.5 %all-gather.8.cloned.1.call-done = f32[512,1024]{1,0:T(8,128)} async-done(((f32[512,128]{1,0:T(8,128)}), f32[512,1024]{1,0:T(8,128)}) %all-gather.8.cloned.1.call-update) | async-done | bytes 2097168 | tf_op jit(solution)/shard_map/all_gather | solution.py:33
  144.5 25.7 %all-to-all-done.1 = f32[8,1024,128]{1,2,0:T(8,128)} async-done(((f32[8,1024,128]{1,2,0:T(8,128)}), f32[8,1024,128]{1,2,0:T(8,128)}, u32[]{:S(2)}, u32[]{:S(2)}) %all-to-all-start.1) | async-done | bytes 4194336 | tf_op jit(solution)/shard_map/all_to_all | solution.py:35
  170.2 0.0 copy-start.1
  170.2 9.8 %fusion.11 = f32[512,1024]{1,0:T(8,128)S(1)} fusion(f32[512,1024]{1,0:T(8,128)} %all-gather.8.cloned.1.call-done, f32[1024,1024]{0,1:T(8,128)} %bitcast.10), kind=kOutput, calls=%fused_computation.34 | convolution fusion | flops 6442450944 | bytes 8388608 | tf_op jit(solution)/shard_map/dot_general | solution.py:36
  180.0 0.0 copy-done.1
  180.0 9.8 %fusion = f32[512,1024]{1,0:T(8,128)} fusion(f32[1024,1024]{0,1:T(8,128)} %bitcast.10, f32[512,1024]{1,0:T(8,128)S(1)} %copy-done.1, f32[512,1024]{1,0:T(8,128)S(1)} %fusion.11), kind=kOutput, calls=%fused_computation.3 | convolution fusion | flops 6442975232 | bytes 10485760 | tf_op jit(solution)/shard_map/dot_general | solution.py:42
  189.8 0.0 all-reduce.2.cloned.1.call-update
  189.8 0.0 all-gather.6.cloned.1.call-start
  189.9 62.2 %all-reduce.2.cloned.1.call-done = f32[512,1024]{1,0:T(8,128)} async-done(((f32[512,1024]{1,0:T(8,128)}), f32[512,1024]{1,0:T(8,128)}) %all-reduce.2.cloned.1.call-update) | async-done | bytes 2097168 | tf_op jit(solution)/shard_map/psum | solution.py:48
  252.1 1.7 constant_dynamic-slice_fusion
  253.7 0.0 all-gather.6.cloned.1.call-update
  253.7 0.0 reduce-scatter.2.cloned.1.call-start
  253.8 52.7 %all-gather.6.cloned.1.call-done = f32[8192,128]{1,0:T(8,128)} async-done(((f32[512,128]{1,0:T(8,128)}), f32[8192,128]{1,0:T(8,128)}) %all-gather.6.cloned.1.call-update) | async-done | bytes 4194320 | tf_op jit(solution)/shard_map/all_gather | solution.py:50
  306.5 5.4 %copy.16 = f32[8,1024,128]{1,2,0:T(8,128)} copy(f32[8,1024,128]{2,1,0:T(8,128)} %bitcast.45) | data formatting | bytes 8388608 | tf_op jit(solution)/shard_map/all_to_all | solution.py:51
  311.9 53.9 %all_to_all.43 = f32[8,1024,128]{1,2,0:T(8,128)S(1)} all-to-all(f32[8,1024,128]{1,2,0:T(8,128)} %copy.16), channel_id=1, replica_groups=mesh['row'=16,'col'=8] {'col'}, dimensions={0} | all-to-all | bytes 8388608 | tf_op jit(solution)/shard_map/all_to_all | solution.py:51
  365.8 29.9 %negate_bitcast_fusion = f32[2048,1024]{0,1:T(8,128)} fusion(f32[1024,1024]{0,1:T(8,128)S(1)} %bitcast.46, f32[2048,1024]{1,0:T(8,128)} %param.7), kind=kOutput, calls=%fused_computation.2 | convolution fusion | flops 25771900928 | bytes 20971520 | tf_op jit(solution)/shard_map/dot_general | solution.py:52
  395.6 0.0 reduce-scatter.2.cloned.1.call-update
  395.7 50.2 %reduce-scatter.2.cloned.1.call-done = f32[2048,128]{0,1:T(8,128)} async-done(((f32[2048,1024]{0,1:T(8,128)}), f32[2048,128]{0,1:T(8,128)}) %reduce-scatter.2.cloned.1.call-update) | async-done | bytes 1048592 | tf_op jit(solution)/shard_map/reduce_scatter | solution.py:55
  445.9 2.5 copy.17
  (9 shorter events, 0.1 us)
Async XLA Ops:
  6.5 21.2 %copy-start = (f32[2048,128]{1,0:T(8,128)S(1)}, f32[2048,128]{1,0:T(8,128)}, u32[]{:S(2)}) copy-start(f32[2048,128]{1,0:T(8,128)} %param.4) | copy-start | bytes 3145732
  31.6 18.0 %all-to-all-start = ((f32[16,64,128]{2,1,0:T(8,128)}), f32[16,64,128]{2,1,0:T(8,128)S(1)}, u32[]{:S(2)}, u32[]{:S(2)}) async-start(f32[16,64,128]{2,1,0:T(8,128)} %broadcast_select_fusion), calls=%async_computation | async-start | bytes 1048576 | tf_op jit(solution)/shard_map/all_to_all | solution.py:28
  39.1 63.2 %all-gather.10.cloned.1.call-start = ((), (), s32[]{:S(2)}) async-start(), calls=%async_computation.8 | async-start | bytes 4456448 | tf_op jit(solution)/shard_map/all_gather | solution.py:34
  51.2 93.3 %all-gather.8.cloned.1.call-start = ((), (), s32[]{:S(2)}) async-start(), calls=%async_computation.7 | async-start | bytes 2359296 | tf_op jit(solution)/shard_map/all_gather | solution.py:33
  107.7 62.5 %all-to-all-start.1 = ((f32[8,1024,128]{1,2,0:T(8,128)}), f32[8,1024,128]{1,2,0:T(8,128)}, u32[]{:S(2)}, u32[]{:S(2)}) async-start(f32[8,1024,128]{1,2,0:T(8,128)} %copy.15), calls=%async_computation.1 | async-start | bytes 8388608 | tf_op jit(solution)/shard_map/all_to_all | solution.py:35
  113.0 139.1 %all-reduce.2.cloned.1.call-start = ((), (), s32[]{:S(2)}) async-start(), calls=%async_computation.4 | async-start | bytes 4194304 | tf_op jit(solution)/shard_map/psum | solution.py:48
  170.2 9.8 %copy-start.1 = (f32[512,1024]{1,0:T(8,128)S(1)}, f32[512,1024]{1,0:T(8,128)}, u32[]{:S(2)}) copy-start(f32[512,1024]{1,0:T(8,128)} %param.6) | copy-start | bytes 6291460
  189.8 116.7 %all-gather.6.cloned.1.call-start = ((), (), s32[]{:S(2)}) async-start(), calls=%async_computation.5 | async-start | bytes 4456448 | tf_op jit(solution)/shard_map/all_gather | solution.py:50
  253.7 192.2 %reduce-scatter.2.cloned.1.call-start = ((), (), s32[]{:S(2)}) async-start(), calls=%async_computation.6 | async-start | bytes 9437184 | tf_op jit(solution)/shard_map/reduce_scatter | solution.py:55
Sparse Core Ops, SparseCore 0:
  51.3 50.9 all-gather.9
  104.0 40.3 all-gather.7
  190.0 62.0 all-reduce.1
  254.1 52.4 all-gather.5
  395.8 50.0 reduce-scatter.1
where the time goes:
time: 456 us; the launch traced here: 455 us
  waiting for transfers between devices  284 us (62%)
  blocking collectives  53.9 us (12%)
  matrix products  49.4 us (11%)
  other arithmetic  21.4 us (5%)
  local copies, waits for them, and re-layouts  20.1 us (4%)
  between operations  13.3 us (3%)
  starting transfers between devices  13 us (3%)
    psum x1, waiting for transfers between devices, per_device(): summed = lax.psum(partial_value, 'col')  62.2 us
    all_to_all x1, blocking collectives, per_device(): lax.all_to_all(weight_all, 'col', split_axis=0, concat_axis=1, tiled=True)  53.9 us
    all_gather x1, waiting for transfers between devices, per_device(): weight_all = lax.all_gather(weight_strip, 'row', axis=0, tiled=True)  52.7 us
    all_gather x1, waiting for transfers between devices, per_device(): strip_all = lax.all_gather(panel_strip, 'row', axis=0, tiled=True)  50.4 us
    reduce_scatter x1, waiting for transfers between devices, per_device(): return lax.psum_scatter(term, 'col', scatter_dimension=1, tiled=True)  50.2 us
    all_gather x1, waiting for transfers between devices, per_device(): panel_full = lax.all_gather(panel_strip, 'col', axis=1, tiled=True)  31.5 us
    dot_general x1, matrix products, per_device(): jnp.dot(fitting, weight_column, precision=lax.Precision.HIGHEST, preferre...  29.9 us
    all_to_all x1, waiting for transfers between devices, per_device(): lax.all_to_all(strip_all, 'col', split_axis=0, concat_axis=1, tiled=True)  25.7 us
  transfers between devices with their start and end apart: 7, of which 7 were waited for; matrix products, arithmetic and copies ran while one was open for 1% of the time, Pallas kernels for 0%

commit v1 on v0

--- a/solution.py
+++ b/solution.py
@@ -47,7 +47,9 @@
     )
     summed = lax.psum(partial_value, "col")
     weight_strip = lax.dynamic_slice_in_dim(summed, my_col * band_cols, band_cols, 1)
-    weight_all = lax.all_gather(weight_strip, "row", axis=0, tiled=True)
+    weight_all = jnp.concatenate(
+        lax.all_to_all(jnp.stack([weight_strip] * lax.axis_size("row")), "row", 0, 0), axis=0
+    )
     weight_column = lax.all_to_all(weight_all, "col", split_axis=0, concat_axis=1, tiled=True)
     term = -jnp.dot(
         fitting, weight_column, precision=lax.Precision.HIGHEST, preferred_element_type=jnp.float32

time: 456 us -> 460 us (level)
  blocking collectives: 53.9 us -> 113 us
  waiting for transfers between devices: 284 us -> 229 us
    all_to_all x0 -> x1, blocking collectives: none -> 54.8 us  [per_device(): lax.all_to_all(jnp.stack([weight_strip] * lax.axis_size('row')), 'row', 0...]
    all_gather x1 -> x0, waiting for transfers between devices: 52.7 us -> none  [per_device(): weight_all = lax.all_gather(weight_strip, 'row', axis=0, tiled=True)]
  transfers between devices with their start and end apart: 7 -> 6, of which waited for: 7 -> 6; matrix products, arithmetic and copies ran while one was open for 1% -> 1% of each run, Pallas kernels for 0% -> 0%
where the time goes in v1:
time: 460 us
  waiting for transfers between devices  229 us (50%)
  blocking collectives  113 us (25%)
  matrix products  50.6 us (11%)
  other arithmetic  21.4 us (5%)
  local copies, waits for them, and re-layouts  19.8 us (4%)
  between operations  13.3 us (3%)
  starting transfers between devices  13 us (3%)
    psum x1, waiting for transfers between devices, per_device(): summed = lax.psum(partial_value, 'col')  62.2 us
    all_to_all x1, blocking collectives, per_device(): lax.all_to_all(weight_all, 'col', split_axis=0, concat_axis=1, tiled=True)  57.9 us
    all_to_all x1, blocking collectives, per_device(): lax.all_to_all(jnp.stack([weight_strip] * lax.axis_size('row')), 'row', 0...  54.8 us
    all_gather x1, waiting for transfers between devices, per_device(): strip_all = lax.all_gather(panel_strip, 'row', axis=0, tiled=True)  50.4 us
    reduce_scatter x1, waiting for transfers between devices, per_device(): return lax.psum_scatter(term, 'col', scatter_dimension=1, tiled=True)  48 us
    all_gather x1, waiting for transfers between devices, per_device(): panel_full = lax.all_gather(panel_strip, 'col', axis=1, tiled=True)  31.5 us
    dot_general x1, matrix products, per_device(): jnp.dot(fitting, weight_column, precision=lax.Precision.HIGHEST, preferre...  31 us
    all_to_all x1, waiting for transfers between devices, per_device(): lax.all_to_all(strip_all, 'col', split_axis=0, concat_axis=1, tiled=True)  25.7 us
  transfers between devices with their start and end apart: 6, of which 6 were waited for; matrix products, arithmetic and copies ran while one was open for 1% of the time, Pallas kernels for 0%

profile of v1, /device:TPU:1, one launch (start us, length us, event | category | flops | bytes accessed | tf_op | source)
XLA Modules:
  0.0 459.6 jit_solution(10626325815664863191)
XLA Ops:
  6.5 0.0 copy-start
  6.5 0.9 add_select_fusion
  7.4 0.1 fusion.6
  7.5 18.1 %reduce-window.6 = s32[16,16,4,128]{3,1,2,0:T(8,128)S(1)} reduce-window(s32[16,16,4,128]{3,1,2,0:T(8,128)S(1)} %fusion.6, s32[]{:T(128)} %constant.16.clone.1), window={size=1x1x1x128 pad=0_0x0_0x0_0x127_0}, to_apply=%region_0.1 | reduce-window | flops 16646144 | bytes 1048580 | tf_op jit(solution)/shard_map/reduce-window
  25.6 0.2 slice.12
  25.9 0.4 copy.17
  26.3 0.1 fusion.8
  26.5 0.2 fusion.5
  26.7 0.4 fusion.3
  27.1 0.5 select_reduce_fusion
  27.7 0.1 reshape.88
  27.7 0.0 copy-done
  27.7 2.8 gather_fusion
  30.6 1.0 broadcast_select_fusion
  31.6 7.6 %all-to-all-start = ((f32[16,64,128]{2,1,0:T(8,128)}), f32[16,64,128]{2,1,0:T(8,128)S(1)}, u32[]{:S(2)}, u32[]{:S(2)}) async-start(f32[16,64,128]{2,1,0:T(8,128)} %broadcast_select_fusion), calls=%async_computation | async-start | bytes 1048576 | tf_op jit(solution)/shard_map/all_to_all | solution.py:28
  39.1 0.0 all-gather.7.cloned.1.call-start
  39.2 10.3 %all-to-all-done = f32[16,64,128]{2,1,0:T(8,128)S(1)} async-done(((f32[16,64,128]{2,1,0:T(8,128)}), f32[16,64,128]{2,1,0:T(8,128)S(1)}, u32[]{:S(2)}, u32[]{:S(2)}) %all-to-all-start) | async-done | bytes 524320 | tf_op jit(solution)/shard_map/all_to_all | solution.py:28
  49.6 1.6 gather_fusion.1
  51.2 0.0 all-gather.7.cloned.1.call-update
  51.2 0.0 all-gather.5.cloned.1.call-start
  51.3 0.7 all-gather.5.cloned.1.call-update
  52.0 50.4 %all-gather.7.cloned.1.call-done = f32[8192,128]{1,0:T(8,128)} async-done(((f32[512,128]{1,0:T(8,128)}), f32[8192,128]{1,0:T(8,128)}) %all-gather.7.cloned.1.call-update) | async-done | bytes 4194320 | tf_op jit(solution)/shard_map/all_gather | solution.py:34
  102.4 5.3 %copy.20 = f32[8,1024,128]{1,2,0:T(8,128)} copy(f32[8,1024,128]{2,1,0:T(8,128)} %bitcast.45) | data formatting | bytes 8388608 | tf_op jit(solution)/shard_map/all_to_all | solution.py:35
  107.7 5.3 %all-to-all-start.1 = ((f32[8,1024,128]{1,2,0:T(8,128)}), f32[8,1024,128]{1,2,0:T(8,128)}, u32[]{:S(2)}, u32[]{:S(2)}) async-start(f32[8,1024,128]{1,2,0:T(8,128)} %copy.20), calls=%async_computation.1 | async-start | bytes 8388608 | tf_op jit(solution)/shard_map/all_to_all | solution.py:35
  113.0 0.0 all-reduce.2.cloned.1.call-start
  113.0 31.5 %all-gather.5.cloned.1.call-done = f32[512,1024]{1,0:T(8,128)} async-done(((f32[512,128]{1,0:T(8,128)}), f32[512,1024]{1,0:T(8,128)}) %all-gather.5.cloned.1.call-update) | async-done | bytes 2097168 | tf_op jit(solution)/shard_map/all_gather | solution.py:33
  144.5 25.7 %all-to-all-done.1 = f32[8,1024,128]{1,2,0:T(8,128)} async-done(((f32[8,1024,128]{1,2,0:T(8,128)}), f32[8,1024,128]{1,2,0:T(8,128)}, u32[]{:S(2)}, u32[]{:S(2)}) %all-to-all-start.1) | async-done | bytes 4194336 | tf_op jit(solution)/shard_map/all_to_all | solution.py:35
  170.2 0.0 copy-start.1
  170.2 9.8 %fusion.11 = f32[512,1024]{1,0:T(8,128)S(1)} fusion(f32[512,1024]{1,0:T(8,128)} %all-gather.5.cloned.1.call-done, f32[1024,1024]{0,1:T(8,128)} %bitcast.10), kind=kOutput, calls=%fused_computation.34 | convolution fusion | flops 6442450944 | bytes 8388608 | tf_op jit(solution)/shard_map/dot_general | solution.py:36
  180.0 0.0 copy-done.1
  180.0 9.8 %fusion = f32[512,1024]{1,0:T(8,128)} fusion(f32[1024,1024]{0,1:T(8,128)} %bitcast.10, f32[512,1024]{1,0:T(8,128)S(1)} %copy-done.1, f32[512,1024]{1,0:T(8,128)S(1)} %fusion.11), kind=kOutput, calls=%fused_computation.3 | convolution fusion | flops 6442975232 | bytes 10485760 | tf_op jit(solution)/shard_map/dot_general | solution.py:42
  189.8 0.0 all-reduce.2.cloned.1.call-update
  189.8 0.0 reduce-scatter.2.cloned.1.call-start
  189.9 62.2 %all-reduce.2.cloned.1.call-done = f32[512,1024]{1,0:T(8,128)} async-done(((f32[512,1024]{1,0:T(8,128)}), f32[512,1024]{1,0:T(8,128)}) %all-reduce.2.cloned.1.call-update) | async-done | bytes 2097168 | tf_op jit(solution)/shard_map/psum | solution.py:48
  252.1 1.0 constant_dynamic-slice_fusion
  253.0 0.4 stack.2
  253.4 54.8 %all_to_all.48 = f32[16,512,128]{2,1,0:T(8,128)S(1)} all-to-all(f32[16,512,128]{2,1,0:T(8,128)S(1)} %stack.2), channel_id=1, replica_groups=mesh['row'=16,'col'=8] {'row'}, dimensions={0} | all-to-all | bytes 8388608 | tf_op jit(solution)/shard_map/all_to_all | solution.py:51
  308.2 57.9 %all_to_all.49 = f32[8,1024,128]{2,1,0:T(8,128)} all-to-all(f32[8,1024,128]{2,1,0:T(8,128)S(1)} %bitcast.42), channel_id=1, replica_groups=mesh['row'=16,'col'=8] {'col'}, dimensions={0} | all-to-all | bytes 8388608 | tf_op jit(solution)/shard_map/all_to_all | solution.py:53
  366.1 5.3 %copy.21 = f32[1024,8,128]{0,2,1:T(8,128)} copy(f32[1024,8,128]{2,0,1:T(8,128)} %bitcast.43) | data formatting | bytes 8388608 | tf_op jit(solution)/shard_map/all_to_all | solution.py:53
  371.5 31.0 %negate_bitcast_fusion = f32[2048,1024]{0,1:T(8,128)} fusion(f32[1024,1024]{0,1:T(8,128)} %bitcast.46, f32[2048,1024]{1,0:T(8,128)} %param.7), kind=kOutput, calls=%fused_computation.2 | convolution fusion | flops 25771900928 | bytes 20971520 | tf_op jit(solution)/shard_map/dot_general | solution.py:54
  402.5 0.0 reduce-scatter.2.cloned.1.call-update
  402.5 48.0 %reduce-scatter.2.cloned.1.call-done = f32[2048,128]{0,1:T(8,128)} async-done(((f32[2048,1024]{0,1:T(8,128)}), f32[2048,128]{0,1:T(8,128)}) %reduce-scatter.2.cloned.1.call-update) | async-done | bytes 1048592 | tf_op jit(solution)/shard_map/reduce_scatter | solution.py:57
  450.5 2.5 copy.22
  (9 shorter events, 0.1 us)
Async XLA Ops:
  6.5 21.2 %copy-start = (f32[2048,128]{1,0:T(8,128)S(1)}, f32[2048,128]{1,0:T(8,128)}, u32[]{:S(2)}) copy-start(f32[2048,128]{1,0:T(8,128)} %param.4) | copy-start | bytes 3145732
  31.6 18.0 %all-to-all-start = ((f32[16,64,128]{2,1,0:T(8,128)}), f32[16,64,128]{2,1,0:T(8,128)S(1)}, u32[]{:S(2)}, u32[]{:S(2)}) async-start(f32[16,64,128]{2,1,0:T(8,128)} %broadcast_select_fusion), calls=%async_computation | async-start | bytes 1048576 | tf_op jit(solution)/shard_map/all_to_all | solution.py:28
  39.1 63.2 %all-gather.7.cloned.1.call-start = ((), (), s32[]{:S(2)}) async-start(), calls=%async_computation.8 | async-start | bytes 4456448 | tf_op jit(solution)/shard_map/all_gather | solution.py:34
  51.2 93.3 %all-gather.5.cloned.1.call-start = ((), (), s32[]{:S(2)}) async-start(), calls=%async_computation.7 | async-start | bytes 2359296 | tf_op jit(solution)/shard_map/all_gather | solution.py:33
  107.7 62.5 %all-to-all-start.1 = ((f32[8,1024,128]{1,2,0:T(8,128)}), f32[8,1024,128]{1,2,0:T(8,128)}, u32[]{:S(2)}, u32[]{:S(2)}) async-start(f32[8,1024,128]{1,2,0:T(8,128)} %copy.20), calls=%async_computation.1 | async-start | bytes 8388608 | tf_op jit(solution)/shard_map/all_to_all | solution.py:35
  113.0 139.1 %all-reduce.2.cloned.1.call-start = ((), (), s32[]{:S(2)}) async-start(), calls=%async_computation.5 | async-start | bytes 4194304 | tf_op jit(solution)/shard_map/psum | solution.py:48
  170.2 9.8 %copy-start.1 = (f32[512,1024]{1,0:T(8,128)S(1)}, f32[512,1024]{1,0:T(8,128)}, u32[]{:S(2)}) copy-start(f32[512,1024]{1,0:T(8,128)} %param.6) | copy-start | bytes 6291460
  189.8 260.7 %reduce-scatter.2.cloned.1.call-start = ((), (), s32[]{:S(2)}) async-start(), calls=%async_computation.6 | async-start | bytes 9437184 | tf_op jit(solution)/shard_map/reduce_scatter | solution.py:57
Sparse Core Ops, SparseCore 0:
  51.3 50.9 all-gather.6
  104.0 40.4 all-gather.4
  190.0 62.0 all-reduce.1
  402.6 47.8 reduce-scatter.1
